TPU v7x, 32 devices: a whole 2x2x4 slice. The times are simulated.
32 devices in a mesh: batch: 2 (over x), seq: 16 (over z, y, core).
Axes of the slice: x: 2, y: 2, z: 4, core: 2. Of those that a mesh axis runs over, the one named last changes fastest.
Arguments:
- inputs: bfloat16 [2, 2048, 1024], P('batch', 'seq'), may hold values from -6 to 6
- seg_ids: int32 [2, 2048], P('batch', 'seq'), may hold values from 0 to 3, never falling along the last dimension, each value on 1 to 1024 neighbouring positions
- gain_attn: bfloat16 [1024], P('batch'), may hold values from 0.5 to 1.5
- w_query: bfloat16 [1024, 512], P('batch'), may hold values from -0.1875 to 0.1875
- w_key: bfloat16 [1024, 512], P('batch'), may hold values from -0.1875 to 0.1875
- w_value: bfloat16 [1024, 1024], P('batch'), may hold values from -0.1875 to 0.1875
- w_outgate: bfloat16 [1024, 1024], P('batch'), may hold values from -0.1875 to 0.1875
- w_rank_in: bfloat16 [1024, 16], P('batch'), may hold values from -0.1875 to 0.1875
- w_rank_out: bfloat16 [16, 512], P(None, 'batch'), may hold values from -1.5 to 1.5
- rank_bias: bfloat16 [512], P('batch'), may hold values from -0.5 to 6
- head_gain: bfloat16 [256], P('batch'), may hold values from 0.5 to 1.5
- w_output: bfloat16 [1024, 1024], P(None, 'batch'), may hold values from -0.1875 to 0.1875
- gain_ffn: bfloat16 [1024], P('batch'), may hold values from 0.5 to 1.5
- w_gate: bfloat16 [1024, 2816], P('batch'), may hold values from -0.1875 to 0.1875
- w_up: bfloat16 [1024, 2816], P('batch'), may hold values from -0.1875 to 0.1875
- w_down: bfloat16 [2816, 1024], P('batch'), may hold values from -0.109375 to 0.109375
- cotangent: bfloat16 [2, 2048, 1024], P('batch', 'seq'), may hold values from -6 to 6
Outputs:
- output: bfloat16 [2, 2048, 1024], P('batch', 'seq')
- grad_inputs: bfloat16 [2, 2048, 1024], P('batch', 'seq')
- grad_gain_attn: float32 [1024], P('batch')
- grad_w_query: float32 [1024, 512], P('batch')
- grad_w_key: float32 [1024, 512], P('batch')
- grad_w_value: float32 [1024, 1024], P('batch')
- grad_w_outgate: float32 [1024, 1024], P('batch')
- grad_w_rank_in: float32 [1024, 16], P('batch')
- grad_w_rank_out: float32 [16, 512], P(None, 'batch')
- grad_rank_bias: float32 [512], P('batch')
- grad_head_gain: float32 [256], P('batch')
- grad_w_output: float32 [1024, 1024], P(None, 'batch')
- grad_gain_ffn: float32 [1024], P('batch')
- grad_w_gate: float32 [1024, 2816], P('batch')
- grad_w_up: float32 [1024, 2816], P('batch')
- grad_w_down: float32 [2816, 1024], P('batch')
Inputs may be any that keep to these rules, and one draw needn't show every extreme that they name: `seg_ids`: along each sequence document ids never fall; each document holds 1 to 1024 tokens and one holds exactly 1024.
All inputs are finite; a program needn't handle non-finite values.
Results may differ from a plain program's by a relative error of at most 0.023.
Values may be sent and summed in bfloat16 or wider, within the bound.
A program may use at most 192 MiB of HBM per device.

v0:
```python
import jax
import jax.numpy as jnp
from jax import lax
from jax.sharding import PartitionSpec as P

HEADS = 4
DK = 128
DV = 256
SPAN = 64
KEYS = 512
VALS = 1024
norm_eps = 1e-05
head_eps = 0.1
top_prec = lax.Precision.HIGHEST
BOTH = ("batch", "seq")


def rms_scale(values_in):
    return lax.rsqrt(jnp.mean(values_in * values_in, axis=-1, keepdims=True) + norm_eps)


def head_rms(values_in):
    return lax.rsqrt(jnp.mean(values_in * values_in, axis=-1, keepdims=True) + head_eps)


def silu_grad(pre_act, sig_val):
    return sig_val * (1.0 + pre_act * (1.0 - sig_val))


def mm(eq, a, b):
    return jnp.einsum(eq, a, b, precision=top_prec)


def own_piece(shard):
    rows = shard.shape[0] // lax.axis_size("seq")
    return lax.dynamic_slice_in_dim(shard, lax.axis_index("seq") * rows, rows, 0)


def gather_rows(shards):
    pieces = [own_piece(shard) for shard in shards]
    piece = pieces[0] if len(pieces) == 1 else jnp.concatenate(pieces, axis=1)
    return lax.all_gather(piece, BOTH, axis=0, tiled=True)


def sum_rows(partial):
    piece = lax.psum_scatter(partial.astype(jnp.bfloat16), BOTH, scatter_dimension=0, tiled=True)
    return lax.all_gather(piece, "seq", axis=0, tiled=True)


def to_spans(array_in, width):
    return array_in.reshape(-1, SPAN, HEADS, width).transpose(0, 2, 1, 3)


def from_spans(array_in):
    spans, heads, span_len, width = array_in.shape
    return array_in.transpose(0, 2, 1, 3).reshape(spans * span_len, heads * width)


def per_device(
    inputs,
    seg_ids,
    gain_attn,
    w_query,
    w_key,
    w_value,
    w_outgate,
    w_rank_in,
    w_rank_out,
    rank_bias,
    head_gain,
    w_output,
    gain_ffn,
    w_gate,
    w_up,
    w_down,
    cotangent,
):
    f32 = jnp.float32
    bf16 = jnp.bfloat16
    nb = lax.axis_size("batch")
    mine_b = lax.axis_index("batch")
    place = lax.axis_index("seq")
    peers = lax.axis_size("seq")
    small = (gain_attn, gain_ffn, rank_bias, head_gain, w_rank_in, w_rank_out)
    packed = jnp.concatenate([a.reshape(-1) for a in small])
    packed = lax.all_gather(packed, "batch", axis=0)
    parts, at = ([], 0)
    for a in small:
        parts.append(packed[:, at : at + a.size])
        at += a.size
    gain_one = parts[0].reshape(-1).astype(f32)
    gain_two = parts[1].reshape(-1).astype(f32)
    bias_w = parts[2].reshape(-1).astype(f32)
    head_gain32 = parts[3].reshape(-1).astype(f32)
    rank_in_w = parts[4].reshape(-1, w_rank_in.shape[1])
    rank_out_w = (
        parts[5]
        .reshape((nb,) + w_rank_out.shape)
        .transpose(1, 0, 2)
        .reshape(w_rank_out.shape[0], -1)
        .astype(f32)
    )
    proj_w = gather_rows((w_query, w_key, w_value, w_outgate))
    output_w = gather_rows((w_output,)).reshape((nb,) + w_output.shape)
    gate_up_w = gather_rows((w_gate, w_up))
    down_w = gather_rows((w_down,))
    ff = w_gate.shape[1]
    activation = inputs[0].astype(f32)
    seg_row = seg_ids[0]
    tok_count = activation.shape[0]
    spans = tok_count // SPAN
    scale_one = rms_scale(activation)
    unit_one = activation * scale_one
    normed = (unit_one * gain_one).astype(bf16)
    low_rank = jnp.dot(normed, rank_in_w, preferred_element_type=f32)
    logits = jnp.dot(low_rank, rank_out_w, precision=top_prec) + bias_w
    decays = jax.nn.log_sigmoid(logits) / 16.0
    seg_s = seg_row.reshape(spans, SPAN)
    first_s, last_s = (seg_s[:, 0], seg_s[:, -1])
    row_pos = lax.broadcasted_iota(jnp.int32, (SPAN, SPAN), 0)
    col_pos = lax.broadcasted_iota(jnp.int32, (SPAN, SPAN), 1)
    lower = (col_pos <= row_pos).astype(f32)
    allowed = lower[None] * (seg_s[:, :, None] == seg_s[:, None, :]).astype(f32)
    allowed = allowed[:, None]
    prior = jnp.concatenate([seg_row[:1], last_s[:-1]])
    enters = (first_s == prior).astype(f32)
    within = ((seg_s == first_s[:, None]).astype(f32) * enters[:, None])[:, None, :, None]
    end_doc = (seg_s == last_s[:, None]).astype(f32)[:, None, :, None]
    cumul = mm("ts,nsc->ntc", lower, decays.reshape(spans, SPAN, KEYS))
    total_log = jnp.sum(cumul[:, -1], axis=0)
    edges = jnp.stack([seg_row[0], seg_row[-1]]).astype(f32)
    notes = lax.all_gather(jnp.concatenate([total_log, edges]), "seq", axis=0)
    all_log, firsts, lasts = (notes[:, :KEYS], notes[:, KEYS], notes[:, KEYS + 1])
    proj = jnp.dot(normed, proj_w, preferred_element_type=f32)
    queries = to_spans(proj[:, :KEYS] * DK ** (-0.5), DK)
    keys_s = to_spans(proj[:, KEYS : 2 * KEYS], DK)
    values_s = to_spans(proj[:, 2 * KEYS : 2 * KEYS + VALS], DV)
    outgate = proj[:, 2 * KEYS + VALS :]
    cumul = cumul.reshape(spans, SPAN, HEADS, DK).transpose(0, 2, 1, 3)
    last_cumul = cumul[:, :, -1:, :]
    grow = jnp.exp(cumul)
    shrink = jnp.exp(-cumul)
    to_end = jnp.exp(last_cumul - cumul) * end_doc
    query_dec = queries * grow
    key_dec = keys_s * shrink
    key_end = keys_s * to_end
    query_in = query_dec * within
    keep = jnp.exp(last_cumul[:, :, 0, :]) * within[:, :, -1]
    scores = mm("nhtc,nhsc->nhts", query_dec, key_dec) * allowed
    local_out = mm("nhts,nhsv->nhtv", scores, values_s)
    added = mm("nhsc,nhsv->nhcv", key_end, values_s)
    local_state = added[0]
    for i in range(1, spans):
        local_state = keep[i][:, :, None] * local_state + added[i]
    states = lax.all_gather(local_state.astype(bf16), "seq", axis=0)
    before = lax.broadcasted_iota(jnp.int32, (peers, peers), 1)
    row = lax.broadcasted_iota(jnp.int32, (peers, peers), 0)
    order = jnp.arange(peers)
    between = jnp.logical_and(before > row, before < place).astype(f32)
    reach = jnp.logical_and(order < place, lasts == edges[0]).astype(f32)
    weight = jnp.exp(mm("ji,ic->jc", between, all_log)) * reach[:, None]
    carried = jnp.sum(states.astype(f32) * weight.reshape(peers, HEADS, DK, 1), axis=0)
    enter_list = [carried]
    for i in range(spans - 1):
        enter_list.append(keep[i][:, :, None] * enter_list[i] + added[i])
    entered = jnp.stack(enter_list)
    attn_raw = from_spans(local_out + mm("nhtc,nhcv->nhtv", query_in, entered)).reshape(
        tok_count, HEADS, DV
    )
    head_scale = head_rms(attn_raw)
    head_norm = attn_raw * head_scale
    gate_h = outgate.reshape(tok_count, HEADS, DV)
    gate_sig = jax.nn.sigmoid(gate_h)
    gate_act = gate_h * gate_sig
    gated = (head_norm * head_gain32 * gate_act).reshape(tok_count, VALS).astype(bf16)
    out_proj = jnp.concatenate(
        [jnp.dot(gated, output_w[b], preferred_element_type=f32) for b in range(nb)], axis=1
    )
    resid = activation + out_proj
    scale_two = rms_scale(resid)
    unit_two = resid * scale_two
    normed_two = (unit_two * gain_two).astype(bf16)
    gate_up = jnp.dot(normed_two, gate_up_w, preferred_element_type=f32)
    gate_pre, up_pre = (gate_up[:, :ff], gate_up[:, ff:])
    ffn_sig = jax.nn.sigmoid(gate_pre)
    hidden = (gate_pre * ffn_sig * up_pre).astype(bf16)
    output = (resid + jnp.dot(hidden, down_w, preferred_element_type=f32)).astype(bf16)
    cot_rows = cotangent[0]
    grad_down = sum_rows(jnp.dot(hidden.T, cot_rows, preferred_element_type=f32))
    grad_hidden = jnp.dot(cot_rows, down_w.T, preferred_element_type=f32)
    grad_gate_up = jnp.concatenate(
        [
            (grad_hidden * up_pre * silu_grad(gate_pre, ffn_sig)).astype(bf16),
            (grad_hidden * gate_pre * ffn_sig).astype(bf16),
        ],
        axis=1,
    )
    grad_gu = sum_rows(jnp.dot(normed_two.T, grad_gate_up, preferred_element_type=f32))
    grad_normed_two = jnp.dot(grad_gate_up, gate_up_w.T, preferred_element_type=f32)
    grad_gain_two = jnp.sum(grad_normed_two * unit_two, axis=0)
    scaled_two = grad_normed_two * gain_two
    grad_resid = cot_rows.astype(f32) + scale_two * (
        scaled_two - unit_two * jnp.mean(scaled_two * unit_two, axis=-1, keepdims=True)
    )
    resid_bf = grad_resid.astype(bf16)
    half = resid_bf.shape[1] // nb
    halves = [resid_bf[:, b * half : (b + 1) * half] for b in range(nb)]
    grad_output = sum_rows(
        jnp.concatenate(
            [jnp.dot(gated.T, part, preferred_element_type=f32) for part in halves], axis=0
        )
    )
    grad_gated = sum(
        (jnp.dot(part, output_w[b].T, preferred_element_type=f32) for b, part in enumerate(halves))
    ).reshape(tok_count, HEADS, DV)
    grad_headgain = jnp.sum(grad_gated * head_norm * gate_act, axis=(0, 1))
    grad_gate_h = grad_gated * head_norm * head_gain32 * silu_grad(gate_h, gate_sig)
    grad_norm_h = grad_gated * head_gain32 * gate_act
    grad_attn = head_scale * (
        grad_norm_h - head_norm * jnp.mean(grad_norm_h * head_norm, axis=-1, keepdims=True)
    )
    grad_o = to_spans(grad_attn.reshape(tok_count, VALS), DV)
    reach_grad = mm("nhtc,nhtv->nhcv", query_in, grad_o)
    local_grad = reach_grad[spans - 1]
    for i in range(spans - 2, -1, -1):
        local_grad = keep[i][:, :, None] * local_grad + reach_grad[i]
    grads_in = lax.all_gather(local_grad.astype(bf16), "seq", axis=0)
    grad_scores = mm("nhtv,nhsv->nhts", grad_o, values_s) * allowed
    grad_qd = mm("nhts,nhsc->nhtc", grad_scores, key_dec)
    grad_qd = grad_qd + within * mm("nhtv,nhcv->nhtc", grad_o, entered)
    grad_kd = mm("nhts,nhtc->nhsc", grad_scores, query_dec)
    grad_v = mm("nhts,nhtv->nhsv", scores, grad_o)
    between = jnp.logical_and(before < row, before > place).astype(f32)
    reach = jnp.logical_and(order > place, firsts == edges[1]).astype(f32)
    weight = jnp.exp(mm("ji,ic->jc", between, all_log)) * reach[:, None]
    grad_end = jnp.sum(grads_in.astype(f32) * weight.reshape(peers, HEADS, DK, 1), axis=0)
    end_list = [grad_end]
    for i in range(spans - 1, 0, -1):
        end_list.append(keep[i][:, :, None] * end_list[-1] + reach_grad[i])
    ends = jnp.stack(end_list[::-1])
    grad_v = grad_v + mm("nhsc,nhcv->nhsv", key_end, ends)
    grad_ke = mm("nhsv,nhcv->nhsc", values_s, ends)
    moved = grad_ke * key_end
    grad_last = jnp.sum(moved, axis=2) + keep * jnp.sum(ends * entered, axis=3)
    grad_cumul = grad_qd * query_dec - grad_kd * key_dec - moved
    grad_d = mm("ts,nhtc->nhsc", lower, grad_cumul) + grad_last[:, :, None, :]
    grad_q = grad_qd * grow
    grad_k = grad_kd * shrink + grad_ke * to_end
    grad_logits = from_spans(grad_d) * jax.nn.sigmoid(-logits) / 16.0
    grad_bias = jnp.sum(grad_logits, axis=0)
    grad_rank_out = jnp.dot(low_rank.T, grad_logits, precision=top_prec)
    grad_low = jnp.dot(grad_logits, rank_out_w.T, precision=top_prec).astype(bf16)
    proj_grad = jnp.concatenate(
        [
            from_spans(grad_q * DK ** (-0.5)).astype(bf16),
            from_spans(grad_k).astype(bf16),
            from_spans(grad_v).astype(bf16),
            grad_gate_h.reshape(tok_count, VALS).astype(bf16),
        ],
        axis=1,
    )
    grad_proj = sum_rows(jnp.dot(normed.T, proj_grad, preferred_element_type=f32))
    grad_normed = jnp.dot(proj_grad, proj_w.T, preferred_element_type=f32) + jnp.dot(
        grad_low, rank_in_w.T, preferred_element_type=f32
    )
    grad_gain_one = jnp.sum(grad_normed * unit_one, axis=0)
    scaled_one = grad_normed * gain_one
    grad_input = (
        grad_resid
        + scale_one
        * (scaled_one - unit_one * jnp.mean(scaled_one * unit_one, axis=-1, keepdims=True))
    ).astype(bf16)
    grad_rank_in = jnp.dot(normed.T, grad_low, preferred_element_type=f32)
    by_owner = jnp.concatenate(
        [
            grad_gain_one.reshape(nb, -1),
            grad_gain_two.reshape(nb, -1),
            grad_bias.reshape(nb, -1),
            grad_headgain.reshape(nb, -1),
            grad_rank_in.reshape(nb, -1),
            grad_rank_out.reshape(w_rank_out.shape[0], nb, -1).transpose(1, 0, 2).reshape(nb, -1),
        ],
        axis=1,
    )
    owned = lax.dynamic_index_in_dim(lax.psum(by_owner, BOTH), mine_b, 0, False)
    outs, at = ([], 0)
    for a in small:
        outs.append(owned[at : at + a.size].reshape(a.shape))
        at += a.size
    g_gain_one, g_gain_two, g_bias, g_headgain, g_rank_in, g_rank_out = outs
    grad_proj = grad_proj.astype(f32)
    grad_gu = grad_gu.astype(f32)
    return (
        output[None],
        grad_input[None],
        g_gain_one,
        grad_proj[:, :KEYS],
        grad_proj[:, KEYS : 2 * KEYS],
        grad_proj[:, 2 * KEYS : 2 * KEYS + VALS],
        grad_proj[:, 2 * KEYS + VALS :],
        g_rank_in,
        g_rank_out,
        g_bias,
        g_headgain,
        grad_output.astype(f32),
        g_gain_two,
        grad_gu[:, :ff],
        grad_gu[:, ff:],
        grad_down.astype(f32),
    )


def solution(mesh):
    in_specs = (
        P("batch", "seq", None),
        P("batch", "seq"),
        P("batch"),
        P("batch", None),
        P("batch", None),
        P("batch", None),
        P("batch", None),
        P("batch", None),
        P(None, "batch"),
        P("batch"),
        P("batch"),
        P(None, "batch"),
        P("batch"),
        P("batch", None),
        P("batch", None),
        P("batch", None),
        P("batch", "seq", None),
    )
    out_specs = (
        P("batch", "seq", None),
        P("batch", "seq", None),
        P("batch"),
        P("batch", None),
        P("batch", None),
        P("batch", None),
        P("batch", None),
        P("batch", None),
        P(None, "batch"),
        P("batch"),
        P("batch"),
        P(None, "batch"),
        P("batch"),
        P("batch", None),
        P("batch", None),
        P("batch", None),
    )
    return jax.shard_map(
        per_device, mesh=mesh, in_specs=in_specs, out_specs=out_specs, check_vma=False
    )
```

profile of v0, /device:TPU:0, one launch (start us, length us, event | category | flops | bytes accessed | tf_op | source)
XLA Modules:
  0.0 1341.5 jit_solution(14421822726846353848)
XLA Ops:
  15.6 5.7 all-gather.2
  32.2 51.4 %all-gather.14.cloned.1.call-done = bf16[1024,3072]{1,0:T(8,128)(2,1)} async-done(((bf16[32,3072]{1,0:T(8,128)(2,1)}), bf16[1024,3072]{1,0:T(8,128)(2,1)}) %all-gather.14.cloned.1.call-update) | async-done | bytes 6291472 | tf_op jit(solution)/shard_map/all_gather | solution.py:42
  83.6 3.8 fusion.128
  89.6 1.7 reshape.398
  91.3 1.7 reshape.392
  93.0 2.1 reshape.399
  95.1 1.8 bitcast_multiply_fusion.4
  97.6 2.1 fusion.51
  108.8 61.4 %all-reduce = f32[8224]{0:T(1024)S(1)} all-reduce(f32[8224]{0:T(1024)S(1)} %maximum_dynamic-update-slice_fusion), channel_id=3, replica_groups=mesh['batch'=2,'seq'=16] {'seq'}, use_global_device_ids=true, to_apply=%add | all-reduce | flops 8224 | bytes 65792
  171.4 2.0 convert_reduce_fusion
  176.1 2.6 fusion.53
  178.6 3.4 multiply_reduce_fusion.1
  187.9 2.1 multiply_convert_fusion.5
  190.0 19.7 %all-gather.18.cloned.1.call-done = bf16[2048,512]{1,0:T(8,128)(2,1)} async-done(((bf16[64,512]{1,0:T(8,128)(2,1)}), bf16[2048,512]{1,0:T(8,128)(2,1)}) %all-gather.18.cloned.1.call-update) | async-done | bytes 2097168 | tf_op jit(solution)/shard_map/all_gather | solution.py:42
  211.3 1.6 fusion.15
  213.1 89.3 %all-gather.20.cloned.1.call-done = bf16[1024,5632]{1,0:T(8,128)(2,1)} async-done(((bf16[32,5632]{1,0:T(8,128)(2,1)}), bf16[1024,5632]{1,0:T(8,128)(2,1)}) %all-gather.20.cloned.1.call-update) | async-done | bytes 11534352 | tf_op jit(solution)/shard_map/all_gather | solution.py:42
  302.4 7.6 fusion.124
  310.0 61.6 %all-gather.22.cloned.1.call-done = bf16[2816,1024]{1,0:T(8,128)(2,1)} async-done(((bf16[88,1024]{1,0:T(8,128)(2,1)}), bf16[2816,1024]{1,0:T(8,128)(2,1)}) %all-gather.22.cloned.1.call-update) | async-done | bytes 5767184 | tf_op jit(solution)/shard_map/all_gather | solution.py:42
  371.7 6.8 multiply_convert_fusion.1
  378.5 4.4 multiply_reduce_fusion.4
  383.9 1.8 fusion.13
  387.0 2.1 reshape.400
  389.1 2.9 multiply_reduce_fusion.3
  392.0 2.1 reshape.401
  394.1 1.6 fusion.37
  403.1 5.3 convolution_convert_fusion.1
  414.0 35.6 %all-gather.24.cloned.1.call-done = bf16[16,4,128,256]{3,2,1,0:T(8,128)(2,1)} async-done(((bf16[1,4,128,256]{3,2,1,0:T(8,128)(2,1)}), bf16[16,4,128,256]{3,2,1,0:T(8,128)(2,1)}) %all-gather.24.cloned.1.call-update) | async-done | bytes 4194320 | tf_op jit(solution)/shard_map/all_gather | solution.py:227
  449.6 3.0 multiply_reduce_fusion
  455.2 1.9 fusion.72
  457.5 4.5 convolution_convert_fusion.2
  463.1 7.1 convolution_convert_fusion
  471.0 118.4 %reduce-scatter.7.cloned.1.call-done = bf16[64,512]{1,0:T(8,128)(2,1)} async-done(((bf16[2048,512]{1,0:T(8,128)(2,1)}), bf16[64,512]{1,0:T(8,128)(2,1)}) %reduce-scatter.7.cloned.1.call-update) | async-done | bytes 65552 | tf_op jit(solution)/shard_map/reduce_scatter | solution.py:46
  590.8 1.6 fusion.4
  593.4 5.1 fusion.90
  600.4 133.6 %reduce-scatter.11.cloned.1.call-done = bf16[88,1024]{1,0:T(8,128)(2,1)} async-done(((bf16[2816,1024]{1,0:T(8,128)(2,1)}), bf16[88,1024]{1,0:T(8,128)(2,1)}) %reduce-scatter.11.cloned.1.call-update) | async-done | bytes 180240 | tf_op jit(solution)/shard_map/reduce_scatter | solution.py:46
  734.1 116.5 %reduce-scatter.5.cloned.1.call-done = bf16[32,3072]{1,0:T(8,128)(2,1)} async-done(((bf16[1024,3072]{1,0:T(8,128)(2,1)}), bf16[32,3072]{1,0:T(8,128)(2,1)}) %reduce-scatter.5.cloned.1.call-update) | async-done | bytes 196624 | tf_op jit(solution)/shard_map/reduce_scatter | solution.py:46
  850.6 156.7 %reduce-scatter.9.cloned.1.call-done = bf16[32,5632]{1,0:T(8,128)(2,1)} async-done(((bf16[1024,5632]{1,0:T(8,128)(2,1)}), bf16[32,5632]{1,0:T(8,128)(2,1)}) %reduce-scatter.9.cloned.1.call-update) | async-done | bytes 360464 | tf_op jit(solution)/shard_map/reduce_scatter | solution.py:46
  1007.3 4.3 fusion.3
  1011.6 34.8 %all-gather.28.cloned.1.call-done = bf16[1024,512]{1,0:T(8,128)(2,1)} async-done(((bf16[64,512]{1,0:T(8,128)(2,1)}), bf16[1024,512]{1,0:T(8,128)(2,1)}) %all-gather.28.cloned.1.call-update) | async-done | bytes 1048592 | tf_op jit(solution)/shard_map/all_gather | solution.py:47
  1046.4 2.8 convert_element_type.216
  1050.3 123.7 %all-reduce.3.cloned.1.call-done = f32[2,13696]{1,0:T(2,128)} async-done(((f32[2,13696]{1,0:T(2,128)}), f32[2,13696]{1,0:T(2,128)}) %all-reduce.3.cloned.1.call-update) | async-done | bytes 109584 | tf_op jit(solution)/shard_map/psum | solution.py:285
  1181.2 39.9 %all-gather.32.cloned.1.call-done = bf16[1408,1024]{1,0:T(8,128)(2,1)} async-done(((bf16[88,1024]{1,0:T(8,128)(2,1)}), bf16[1408,1024]{1,0:T(8,128)(2,1)}) %all-gather.32.cloned.1.call-update) | async-done | bytes 2883600 | tf_op jit(solution)/shard_map/all_gather | solution.py:47
  1221.2 5.1 convert_element_type.220
  1226.3 41.2 %all-gather.26.cloned.1.call-done = bf16[512,3072]{1,0:T(8,128)(2,1)} async-done(((bf16[32,3072]{1,0:T(8,128)(2,1)}), bf16[512,3072]{1,0:T(8,128)(2,1)}) %all-gather.26.cloned.1.call-update) | async-done | bytes 3145744 | tf_op jit(solution)/shard_map/all_gather | solution.py:47
  1267.4 3.0 fusion.137
  1270.4 2.5 fusion.136
  1272.9 53.7 %all-gather.30.cloned.1.call-done = bf16[512,5632]{1,0:T(8,128)(2,1)} async-done(((bf16[32,5632]{1,0:T(8,128)(2,1)}), bf16[512,5632]{1,0:T(8,128)(2,1)}) %all-gather.30.cloned.1.call-update) | async-done | bytes 5767184 | tf_op jit(solution)/shard_map/all_gather | solution.py:47
  1326.6 8.1 fusion.135
  (336 shorter events, 73.4 us)
Async XLA Ops:
  7.2 97.9 %copy-start = (bf16[1408,1024]{1,0:T(8,128)(2,1)S(1)}, bf16[1408,1024]{1,0:T(8,128)(2,1)}, u32[]{:S(2)}) copy-start(bf16[1408,1024]{1,0:T(8,128)(2,1)} %param.32) | copy-start | bytes 8650756
  7.2 21.2 %copy-start.78 = (s32[1,128]{1,0:T(1,128)S(1)}, s32[1,128]{1,0:T(1,128)}, u32[]{:S(2)}) copy-start(s32[1,128]{1,0:T(1,128)} %param.18) | copy-start | bytes 1540
  7.2 76.4 %copy-start.3 = (bf16[1,128,1024]{2,1,0:T(8,128)(2,1)S(1)}, bf16[1,128,1024]{2,1,0:T(8,128)(2,1)}, u32[]{:S(2)}) copy-start(bf16[1,128,1024]{2,1,0:T(8,128)(2,1)} %param.17) | copy-start | bytes 786436
  7.2 76.3 %all-gather.14.cloned.1.call-start = ((), (), s32[]{:S(2)}) async-start(), calls=%async_computation.4 | async-start | bytes 6488064 | tf_op jit(solution)/shard_map/all_gather | solution.py:42
  9.8 168.8 %all-gather.16.cloned.1.call-start = ((), (), s32[]{:S(2)}) async-start(), calls=%async_computation.5 | async-start | bytes 4456448 | tf_op jit(solution)/shard_map/all_gather | solution.py:155
  23.7 4.7 copy-start.58
  24.9 62.5 %copy-start.62 = (f32[128]{0:T(128)}, f32[128]{0:T(128)S(1)}, u32[]{:S(2)}) copy-start(f32[128]{0:T(128)S(1)} %add_rsqrt_fusion.2) | copy-start | bytes 1540
  28.4 66.7 %copy-start.56 = (f32[2,4,1,128]{3,2,1,0:T(1,128)}, f32[2,4,1,128]{3,2,1,0:T(1,128)S(1)}, u32[]{:S(2)}) copy-start(f32[2,4,1,128]{3,2,1,0:T(1,128)S(1)} %slice.232) | copy-start | bytes 12292
  31.6 63.5 %copy-start.72 = (f32[2,64]{1,0:T(2,128)}, f32[2,64]{1,0:T(2,128)S(1)}, u32[]{:S(2)}) copy-start(f32[2,64]{1,0:T(2,128)S(1)} %compare_convert_fusion) | copy-start | bytes 1540
  32.2 67.6 %copy-start.66 = (f32[4,128]{1,0:T(4,128)}, f32[4,128]{1,0:T(4,128)S(1)}, u32[]{:S(2)}) copy-start(f32[4,128]{1,0:T(4,128)S(1)} %get-tuple-element.116) | copy-start | bytes 6148
  97.6 8.4 copy-start.81
  97.6 75.9 %copy-start.75 = (s32[2]{0:T(128)S(1)}, s32[2]{0:T(128)}, u32[]{:S(2)}) copy-start(s32[2]{0:T(128)} %copy-done.74) | copy-start | bytes 28
  101.6 108.1 %all-gather.18.cloned.1.call-start = ((), (), s32[]{:S(2)}) async-start(), calls=%async_computation.6 | async-start | bytes 2162688 | tf_op jit(solution)/shard_map/all_gather | solution.py:42
  103.2 199.3 %all-gather.20.cloned.1.call-start = ((), (), s32[]{:S(2)}) async-start(), calls=%async_computation.7 | async-start | bytes 11894784 | tf_op jit(solution)/shard_map/all_gather | solution.py:42
  105.0 266.6 %all-gather.22.cloned.1.call-start = ((), (), s32[]{:S(2)}) async-start(), calls=%async_computation.8 | async-start | bytes 5947392 | tf_op jit(solution)/shard_map/all_gather | solution.py:42
  105.8 343.8 %all-gather.24.cloned.1.call-start = ((), (), s32[]{:S(2)}) async-start(), calls=%async_computation.9 | async-start | bytes 4456448 | tf_op jit(solution)/shard_map/all_gather | solution.py:227
  173.6 223.7 %copy-start.69 = (f32[2,64]{1,0:T(2,128)}, f32[2,64]{1,0:T(2,128)S(1)}, u32[]{:S(2)}) copy-start(f32[2,64]{1,0:T(2,128)S(1)} %compare_select_fusion.3) | copy-start | bytes 1540
  176.1 6.0 copy-start.17
  183.8 6.2 copy-start.9
  213.1 169.8 %copy-start.64 = (f32[128]{0:T(128)}, f32[128]{0:T(128)S(1)}, u32[]{:S(2)}) copy-start(f32[128]{0:T(128)S(1)} %add_rsqrt_fusion.1) | copy-start | bytes 1540
  371.7 6.8 copy-start.2
  378.5 4.4 copy-start.28
  378.5 5.2 copy-start.34
  395.8 4.7 copy-start.33
  395.8 4.7 copy-start.39
  400.4 189.0 %reduce-scatter.7.cloned.1.call-start = ((), (), s32[]{:S(2)}) async-start(), calls=%async_computation.13 | async-start | bytes 2162688 | tf_op jit(solution)/shard_map/reduce_scatter | solution.py:46
  402.9 331.2 %reduce-scatter.11.cloned.1.call-start = ((), (), s32[]{:S(2)}) async-start(), calls=%async_computation.17 | async-start | bytes 5947392 | tf_op jit(solution)/shard_map/reduce_scatter | solution.py:46
  408.5 442.1 %reduce-scatter.5.cloned.1.call-start = ((), (), s32[]{:S(2)}) async-start(), calls=%async_computation.11 | async-start | bytes 6488064 | tf_op jit(solution)/shard_map/reduce_scatter | solution.py:46
  412.6 40.1 %copy-start.67 = (f32[4,128]{1,0:T(4,128)S(1)}, f32[4,128]{1,0:T(4,128)}, u32[]{:S(2)}) copy-start(f32[4,128]{1,0:T(4,128)} %copy-done.66) | copy-start | bytes 6148
  457.3 4.7 copy-start.49
  457.5 4.5 copy-start.51
  462.1 545.2 %reduce-scatter.9.cloned.1.call-start = ((), (), s32[]{:S(2)}) async-start(), calls=%async_computation.15 | async-start | bytes 11894784 | tf_op jit(solution)/shard_map/reduce_scatter | solution.py:46
  470.3 119.4 %copy-start.13 = (f32[1,4,128,256]{3,2,1,0:T(8,128)S(1)}, f32[1,4,128,256]{3,2,1,0:T(8,128)}, u32[]{:S(2)}) copy-start(f32[1,4,128,256]{3,2,1,0:T(8,128)} %copy-done.11) | copy-start | bytes 1572868
  470.3 119.4 %copy-start.15 = (f32[1,4,128,256]{3,2,1,0:T(8,128)S(1)}, f32[1,4,128,256]{3,2,1,0:T(8,128)}, u32[]{:S(2)}) copy-start(f32[1,4,128,256]{3,2,1,0:T(8,128)} %copy-done.14) | copy-start | bytes 1572868
  470.3 119.7 %copy-start.77 = (f32[2]{0:T(128)S(1)}, f32[2]{0:T(128)}, u32[]{:S(2)}) copy-start(f32[2]{0:T(128)} %copy-done.76) | copy-start | bytes 28
  470.3 122.4 %copy-start.59 = (bf16[2,8,2,256]{3,1,2,0:T(8,128)(2,1)S(1)}, bf16[2,8,2,256]{3,1,2,0:T(8,128)(2,1)}, u32[]{:S(2)}) copy-start(bf16[2,8,2,256]{3,1,2,0:T(8,128)(2,1)} %copy-done.58) | copy-start | bytes 49156
  470.3 576.1 %all-gather.28.cloned.1.call-start = ((), (), s32[]{:S(2)}) async-start(), calls=%async_computation.14 | async-start | bytes 1114112 | tf_op jit(solution)/shard_map/all_gather | solution.py:47
  589.4 584.6 %all-reduce.3.cloned.1.call-start = ((), (), s32[]{:S(2)}) async-start(), calls=%async_computation.10 | async-start | bytes 219136 | tf_op jit(solution)/shard_map/psum | solution.py:285
  593.4 5.2 copy-start.32
  593.4 5.6 copy-start.61
  598.6 408.8 %copy-start.23 = (bf16[128,2816]{1,0:T(8,128)(2,1)S(1)}, bf16[128,2816]{1,0:T(8,128)(2,1)}, u32[]{:S(2)}) copy-start(bf16[128,2816]{1,0:T(8,128)(2,1)} %get-tuple-element.102) | copy-start | bytes 2162692
  600.3 620.9 %all-gather.32.cloned.1.call-start = ((), (), s32[]{:S(2)}) async-start(), calls=%async_computation.18 | async-start | bytes 3063808 | tf_op jit(solution)/shard_map/all_gather | solution.py:47
  734.1 533.4 %all-gather.26.cloned.1.call-start = ((), (), s32[]{:S(2)}) async-start(), calls=%async_computation.12 | async-start | bytes 3342336 | tf_op jit(solution)/shard_map/all_gather | solution.py:47
  850.6 476.0 %all-gather.30.cloned.1.call-start = ((), (), s32[]{:S(2)}) async-start(), calls=%async_computation.16 | async-start | bytes 6127616 | tf_op jit(solution)/shard_map/all_gather | solution.py:47
  1011.6 37.6 %copy-start.25 = (f32[128,1024]{1,0:T(8,128)S(1)}, f32[128,1024]{1,0:T(8,128)}, u32[]{:S(2)}) copy-start(f32[128,1024]{1,0:T(8,128)} %copy-done.24) | copy-start | bytes 1572868
  1011.6 37.6 %copy-start.36 = (bf16[1,128,1024]{2,1,0:T(8,128)(2,1)S(1)}, bf16[1,128,1024]{2,1,0:T(8,128)(2,1)}, u32[]{:S(2)}) copy-start(bf16[1,128,1024]{2,1,0:T(8,128)(2,1)} %param.33) | copy-start | bytes 786436
  1011.6 37.6 %copy-start.80 = (f32[128]{0:T(128)S(1)}, f32[128]{0:T(128)}, u32[]{:S(2)}) copy-start(f32[128]{0:T(128)} %copy-done.79) | copy-start | bytes 1540
  1326.6 8.1 copy-start.1
  (49 other events, 115.0 us)
Sparse Core Ops, SparseCore 0:
  11.5 72.0 all-gather.13
  101.7 49.5 all-gather.15
  154.8 54.8 all-gather.17
  213.0 89.3 all-gather.19
  305.7 65.8 all-gather.21
  400.5 49.0 all-gather.23
  452.4 136.8 reduce-scatter.6
  592.2 141.7 reduce-scatter.10
  739.7 110.8 reduce-scatter.4
  852.7 154.5 reduce-scatter.8
  1009.5 36.8 all-gather.27
  1052.4 121.5 all-reduce.2
  1176.3 44.8 all-gather.31
  1223.3 44.0 all-gather.25
  1269.6 56.9 all-gather.29
where the time goes:
time: 1350 us; the launch traced here: 1340 us
  waiting for transfers between devices  1080 us (80%)
  matrix products  79.5 us (6%)
  blocking collectives  67.1 us (5%)
  local copies, waits for them, and re-layouts  60.4 us (4%)
  other arithmetic  41 us (3%)
  between operations  16.1 us (1%)
    reduce_scatter x4, waiting for transfers between devices, sum_rows(): lax.psum_scatter(partial.astype(jnp.bfloat16), BOTH, scatter_dimension=0,...  525 us
    all_gather x4, waiting for transfers between devices, gather_rows(): return lax.all_gather(piece, BOTH, axis=0, tiled=True)  222 us
    all_gather x4, waiting for transfers between devices, sum_rows(): return lax.all_gather(piece, 'seq', axis=0, tiled=True)  170 us
    psum x1, waiting for transfers between devices, per_device(): owned = lax.dynamic_index_in_dim(lax.psum(by_owner, BOTH), mine_b, 0, False)  124 us
    unnamed x1, blocking collectives  61.4 us
    all_gather x1, waiting for transfers between devices, per_device(): grads_in = lax.all_gather(local_grad.astype(bf16), 'seq', axis=0)  35.6 us
  transfers between devices with their start and end apart: 15, of which 14 were waited for; matrix products, arithmetic and copies ran while one was open for 9% of the time, Pallas kernels for 0%

commit v1 on v0

--- a/solution.py
+++ b/solution.py
@@ -282,7 +282,9 @@
         ],
         axis=1,
     )
-    owned = lax.dynamic_index_in_dim(lax.psum(by_owner, BOTH), mine_b, 0, False)
+    owned = lax.dynamic_index_in_dim(
+        jnp.sum(lax.all_gather(by_owner, BOTH), axis=0), mine_b, 0, False
+    )
     outs, at = ([], 0)
     for a in small:
         outs.append(owned[at : at + a.size].reshape(a.shape))

time: 1350 us -> 1280 us (0.948)
  waiting for transfers between devices: 1080 us -> 1010 us
    psum x1 -> x0, waiting for transfers between devices: 124 us -> none  [per_device(): owned = lax.dynamic_index_in_dim(lax.psum(by_owner, BOTH), mine_b, 0, False)]
    all_gather x0 -> x1, waiting for transfers between devices: none -> 58.6 us  [per_device(): lax.all_gather(by_owner, BOTH)]
where the time goes in v1:
time: 1280 us; the launch traced here: 1270 us
  waiting for transfers between devices  1010 us (79%)
  matrix products  79.5 us (6%)
  blocking collectives  67.1 us (5%)
  local copies, waits for them, and re-layouts  56.8 us (4%)
  other arithmetic  44.1 us (3%)
  between operations  16.1 us (1%)
    reduce_scatter x4, waiting for transfers between devices, sum_rows(): lax.psum_scatter(partial.astype(jnp.bfloat16), BOTH, scatter_dimension=0,...  525 us
    all_gather x4, waiting for transfers between devices, gather_rows(): return lax.all_gather(piece, BOTH, axis=0, tiled=True)  222 us
    all_gather x4, waiting for transfers between devices, sum_rows(): return lax.all_gather(piece, 'seq', axis=0, tiled=True)  168 us
    unnamed x1, blocking collectives  61.4 us
    all_gather x1, waiting for transfers between devices, per_device(): lax.all_gather(by_owner, BOTH)  58.6 us
    all_gather x1, waiting for transfers between devices, per_device(): grads_in = lax.all_gather(local_grad.astype(bf16), 'seq', axis=0)  35.6 us
  transfers between devices with their start and end apart: 15, of which 14 were waited for; matrix products, arithmetic and copies ran while one was open for 9% of the time, Pallas kernels for 0%

profile of v1, /device:TPU:0, one launch (start us, length us, event | category | flops | bytes accessed | tf_op | source)
XLA Modules:
  0.0 1273.8 jit_solution(15487395174602288925)
XLA Ops:
  15.6 5.7 all-gather.3
  32.2 51.4 %all-gather.17.cloned.1.call-done = bf16[1024,3072]{1,0:T(8,128)(2,1)} async-done(((bf16[32,3072]{1,0:T(8,128)(2,1)}), bf16[1024,3072]{1,0:T(8,128)(2,1)}) %all-gather.17.cloned.1.call-update) | async-done | bytes 6291472 | tf_op jit(solution)/shard_map/all_gather | solution.py:42
  83.6 3.8 fusion.128
  89.5 1.7 reshape.398
  91.3 1.7 reshape.392
  93.0 2.1 reshape.399
  95.1 1.8 bitcast_multiply_fusion.4
  97.6 2.1 fusion.51
  108.8 61.4 %all-reduce = f32[8224]{0:T(1024)S(1)} all-reduce(f32[8224]{0:T(1024)S(1)} %maximum_dynamic-update-slice_fusion), channel_id=3, replica_groups=mesh['batch'=2,'seq'=16] {'seq'}, use_global_device_ids=true, to_apply=%add | all-reduce | flops 8224 | bytes 65792
  171.4 2.1 convert_reduce_fusion
  176.1 2.6 fusion.53
  178.7 3.4 multiply_reduce_fusion.1
  188.0 2.1 multiply_convert_fusion.5
  190.1 19.5 %all-gather.21.cloned.1.call-done = bf16[2048,512]{1,0:T(8,128)(2,1)} async-done(((bf16[64,512]{1,0:T(8,128)(2,1)}), bf16[2048,512]{1,0:T(8,128)(2,1)}) %all-gather.21.cloned.1.call-update) | async-done | bytes 2097168 | tf_op jit(solution)/shard_map/all_gather | solution.py:42
  213.1 89.3 %all-gather.23.cloned.1.call-done = bf16[1024,5632]{1,0:T(8,128)(2,1)} async-done(((bf16[32,5632]{1,0:T(8,128)(2,1)}), bf16[1024,5632]{1,0:T(8,128)(2,1)}) %all-gather.23.cloned.1.call-update) | async-done | bytes 11534352 | tf_op jit(solution)/shard_map/all_gather | solution.py:42
  302.4 7.6 fusion.124
  310.0 61.6 %all-gather.25.cloned.1.call-done = bf16[2816,1024]{1,0:T(8,128)(2,1)} async-done(((bf16[88,1024]{1,0:T(8,128)(2,1)}), bf16[2816,1024]{1,0:T(8,128)(2,1)}) %all-gather.25.cloned.1.call-update) | async-done | bytes 5767184 | tf_op jit(solution)/shard_map/all_gather | solution.py:42
  371.6 6.8 multiply_convert_fusion.1
  378.5 4.4 multiply_reduce_fusion.4
  383.9 1.8 fusion.13
  387.0 2.1 reshape.400
  389.1 2.9 multiply_reduce_fusion.3
  392.0 2.1 reshape.401
  394.1 1.6 fusion.37
  403.1 5.3 convolution_convert_fusion.1
  414.0 35.6 %all-gather.27.cloned.1.call-done = bf16[16,4,128,256]{3,2,1,0:T(8,128)(2,1)} async-done(((bf16[1,4,128,256]{3,2,1,0:T(8,128)(2,1)}), bf16[16,4,128,256]{3,2,1,0:T(8,128)(2,1)}) %all-gather.27.cloned.1.call-update) | async-done | bytes 4194320 | tf_op jit(solution)/shard_map/all_gather | solution.py:227
  449.7 3.0 multiply_reduce_fusion
  455.3 1.9 fusion.72
  457.6 4.5 convolution_convert_fusion.2
  463.2 7.1 convolution_convert_fusion
  471.0 118.4 %reduce-scatter.7.cloned.1.call-done = bf16[64,512]{1,0:T(8,128)(2,1)} async-done(((bf16[2048,512]{1,0:T(8,128)(2,1)}), bf16[64,512]{1,0:T(8,128)(2,1)}) %reduce-scatter.7.cloned.1.call-update) | async-done | bytes 65552 | tf_op jit(solution)/shard_map/reduce_scatter | solution.py:46
  590.9 1.6 fusion.4
  593.4 5.1 fusion.90
  600.4 133.4 %reduce-scatter.11.cloned.1.call-done = bf16[88,1024]{1,0:T(8,128)(2,1)} async-done(((bf16[2816,1024]{1,0:T(8,128)(2,1)}), bf16[88,1024]{1,0:T(8,128)(2,1)}) %reduce-scatter.11.cloned.1.call-update) | async-done | bytes 180240 | tf_op jit(solution)/shard_map/reduce_scatter | solution.py:46
  733.9 116.5 %reduce-scatter.5.cloned.1.call-done = bf16[32,3072]{1,0:T(8,128)(2,1)} async-done(((bf16[1024,3072]{1,0:T(8,128)(2,1)}), bf16[32,3072]{1,0:T(8,128)(2,1)}) %reduce-scatter.5.cloned.1.call-update) | async-done | bytes 196624 | tf_op jit(solution)/shard_map/reduce_scatter | solution.py:46
  850.5 156.3 %reduce-scatter.9.cloned.1.call-done = bf16[32,5632]{1,0:T(8,128)(2,1)} async-done(((bf16[1024,5632]{1,0:T(8,128)(2,1)}), bf16[32,5632]{1,0:T(8,128)(2,1)}) %reduce-scatter.9.cloned.1.call-update) | async-done | bytes 360464 | tf_op jit(solution)/shard_map/reduce_scatter | solution.py:46
  1006.9 4.3 fusion.3
  1011.1 34.8 %all-gather.31.cloned.1.call-done = bf16[1024,512]{1,0:T(8,128)(2,1)} async-done(((bf16[64,512]{1,0:T(8,128)(2,1)}), bf16[1024,512]{1,0:T(8,128)(2,1)}) %all-gather.31.cloned.1.call-update) | async-done | bytes 1048592 | tf_op jit(solution)/shard_map/all_gather | solution.py:47
  1046.0 2.8 convert_element_type.216
  1049.8 58.6 %all-gather.37.cloned.1.call-done = f32[32,2,13696]{2,1,0:T(2,128)} async-done(((f32[1,2,13696]{2,1,0:T(2,128)}), f32[32,2,13696]{2,1,0:T(2,128)}) %all-gather.37.cloned.1.call-update) | async-done | bytes 3506192 | tf_op jit(solution)/shard_map/all_gather | solution.py:286
  1108.4 3.0 reduce_sum.177
  1115.0 38.5 %all-gather.35.cloned.1.call-done = bf16[1408,1024]{1,0:T(8,128)(2,1)} async-done(((bf16[88,1024]{1,0:T(8,128)(2,1)}), bf16[1408,1024]{1,0:T(8,128)(2,1)}) %all-gather.35.cloned.1.call-update) | async-done | bytes 2883600 | tf_op jit(solution)/shard_map/all_gather | solution.py:47
  1153.5 5.1 convert_element_type.220
  1158.6 41.2 %all-gather.29.cloned.1.call-done = bf16[512,3072]{1,0:T(8,128)(2,1)} async-done(((bf16[32,3072]{1,0:T(8,128)(2,1)}), bf16[512,3072]{1,0:T(8,128)(2,1)}) %all-gather.29.cloned.1.call-update) | async-done | bytes 3145744 | tf_op jit(solution)/shard_map/all_gather | solution.py:47
  1199.8 3.0 fusion.137
  1202.7 2.5 fusion.136
  1205.2 53.7 %all-gather.33.cloned.1.call-done = bf16[512,5632]{1,0:T(8,128)(2,1)} async-done(((bf16[32,5632]{1,0:T(8,128)(2,1)}), bf16[512,5632]{1,0:T(8,128)(2,1)}) %all-gather.33.cloned.1.call-update) | async-done | bytes 5767184 | tf_op jit(solution)/shard_map/all_gather | solution.py:47
  1258.9 8.1 fusion.135
  (337 shorter events, 71.4 us)
Async XLA Ops:
  7.2 97.9 %copy-start = (bf16[1408,1024]{1,0:T(8,128)(2,1)S(1)}, bf16[1408,1024]{1,0:T(8,128)(2,1)}, u32[]{:S(2)}) copy-start(bf16[1408,1024]{1,0:T(8,128)(2,1)} %param.32) | copy-start | bytes 8650756
  7.2 21.2 %copy-start.78 = (s32[1,128]{1,0:T(1,128)S(1)}, s32[1,128]{1,0:T(1,128)}, u32[]{:S(2)}) copy-start(s32[1,128]{1,0:T(1,128)} %param.18) | copy-start | bytes 1540
  7.2 76.3 %copy-start.3 = (bf16[1,128,1024]{2,1,0:T(8,128)(2,1)S(1)}, bf16[1,128,1024]{2,1,0:T(8,128)(2,1)}, u32[]{:S(2)}) copy-start(bf16[1,128,1024]{2,1,0:T(8,128)(2,1)} %param.17) | copy-start | bytes 786436
  7.2 76.3 %all-gather.17.cloned.1.call-start = ((), (), s32[]{:S(2)}) async-start(), calls=%async_computation.4 | async-start | bytes 6488064 | tf_op jit(solution)/shard_map/all_gather | solution.py:42
  9.8 168.9 %all-gather.19.cloned.1.call-start = ((), (), s32[]{:S(2)}) async-start(), calls=%async_computation.5 | async-start | bytes 4456448 | tf_op jit(solution)/shard_map/all_gather | solution.py:155
  23.7 4.7 copy-start.58
  24.9 62.5 %copy-start.62 = (f32[128]{0:T(128)}, f32[128]{0:T(128)S(1)}, u32[]{:S(2)}) copy-start(f32[128]{0:T(128)S(1)} %add_rsqrt_fusion.2) | copy-start | bytes 1540
  28.4 66.7 %copy-start.56 = (f32[2,4,1,128]{3,2,1,0:T(1,128)}, f32[2,4,1,128]{3,2,1,0:T(1,128)S(1)}, u32[]{:S(2)}) copy-start(f32[2,4,1,128]{3,2,1,0:T(1,128)S(1)} %slice.232) | copy-start | bytes 12292
  31.6 63.5 %copy-start.72 = (f32[2,64]{1,0:T(2,128)}, f32[2,64]{1,0:T(2,128)S(1)}, u32[]{:S(2)}) copy-start(f32[2,64]{1,0:T(2,128)S(1)} %compare_convert_fusion) | copy-start | bytes 1540
  32.2 67.6 %copy-start.66 = (f32[4,128]{1,0:T(4,128)}, f32[4,128]{1,0:T(4,128)S(1)}, u32[]{:S(2)}) copy-start(f32[4,128]{1,0:T(4,128)S(1)} %get-tuple-element.116) | copy-start | bytes 6148
  97.6 8.4 copy-start.81
  97.6 76.1 %copy-start.75 = (s32[2]{0:T(128)S(1)}, s32[2]{0:T(128)}, u32[]{:S(2)}) copy-start(s32[2]{0:T(128)} %copy-done.74) | copy-start | bytes 28
  101.6 108.1 %all-gather.21.cloned.1.call-start = ((), (), s32[]{:S(2)}) async-start(), calls=%async_computation.6 | async-start | bytes 2162688 | tf_op jit(solution)/shard_map/all_gather | solution.py:42
  103.2 199.2 %all-gather.23.cloned.1.call-start = ((), (), s32[]{:S(2)}) async-start(), calls=%async_computation.7 | async-start | bytes 11894784 | tf_op jit(solution)/shard_map/all_gather | solution.py:42
  105.0 266.6 %all-gather.25.cloned.1.call-start = ((), (), s32[]{:S(2)}) async-start(), calls=%async_computation.8 | async-start | bytes 5947392 | tf_op jit(solution)/shard_map/all_gather | solution.py:42
  105.8 343.8 %all-gather.27.cloned.1.call-start = ((), (), s32[]{:S(2)}) async-start(), calls=%async_computation.9 | async-start | bytes 4456448 | tf_op jit(solution)/shard_map/all_gather | solution.py:227
  173.8 223.6 %copy-start.69 = (f32[2,64]{1,0:T(2,128)}, f32[2,64]{1,0:T(2,128)S(1)}, u32[]{:S(2)}) copy-start(f32[2,64]{1,0:T(2,128)S(1)} %compare_select_fusion.3) | copy-start | bytes 1540
  176.1 6.0 copy-start.17
  183.9 6.2 copy-start.9
  213.1 169.8 %copy-start.64 = (f32[128]{0:T(128)}, f32[128]{0:T(128)S(1)}, u32[]{:S(2)}) copy-start(f32[128]{0:T(128)S(1)} %add_rsqrt_fusion.1) | copy-start | bytes 1540
  371.6 6.8 copy-start.2
  378.5 4.4 copy-start.28
  378.5 5.2 copy-start.34
  395.8 4.7 copy-start.33
  395.8 4.7 copy-start.39
  400.4 189.0 %reduce-scatter.7.cloned.1.call-start = ((), (), s32[]{:S(2)}) async-start(), calls=%async_computation.12 | async-start | bytes 2162688 | tf_op jit(solution)/shard_map/reduce_scatter | solution.py:46
  402.9 330.9 %reduce-scatter.11.cloned.1.call-start = ((), (), s32[]{:S(2)}) async-start(), calls=%async_computation.16 | async-start | bytes 5947392 | tf_op jit(solution)/shard_map/reduce_scatter | solution.py:46
  408.5 441.9 %reduce-scatter.5.cloned.1.call-start = ((), (), s32[]{:S(2)}) async-start(), calls=%async_computation.10 | async-start | bytes 6488064 | tf_op jit(solution)/shard_map/reduce_scatter | solution.py:46
  412.6 40.1 %copy-start.67 = (f32[4,128]{1,0:T(4,128)S(1)}, f32[4,128]{1,0:T(4,128)}, u32[]{:S(2)}) copy-start(f32[4,128]{1,0:T(4,128)} %copy-done.66) | copy-start | bytes 6148
  457.4 4.7 copy-start.49
  457.5 4.5 copy-start.51
  462.1 544.7 %reduce-scatter.9.cloned.1.call-start = ((), (), s32[]{:S(2)}) async-start(), calls=%async_computation.14 | async-start | bytes 11894784 | tf_op jit(solution)/shard_map/reduce_scatter | solution.py:46
  470.3 119.4 %copy-start.13 = (f32[1,4,128,256]{3,2,1,0:T(8,128)S(1)}, f32[1,4,128,256]{3,2,1,0:T(8,128)}, u32[]{:S(2)}) copy-start(f32[1,4,128,256]{3,2,1,0:T(8,128)} %copy-done.11) | copy-start | bytes 1572868
  470.3 119.4 %copy-start.15 = (f32[1,4,128,256]{3,2,1,0:T(8,128)S(1)}, f32[1,4,128,256]{3,2,1,0:T(8,128)}, u32[]{:S(2)}) copy-start(f32[1,4,128,256]{3,2,1,0:T(8,128)} %copy-done.14) | copy-start | bytes 1572868
  470.3 119.7 %copy-start.77 = (f32[2]{0:T(128)S(1)}, f32[2]{0:T(128)}, u32[]{:S(2)}) copy-start(f32[2]{0:T(128)} %copy-done.76) | copy-start | bytes 28
  470.4 122.4 %copy-start.59 = (bf16[2,8,2,256]{3,1,2,0:T(8,128)(2,1)S(1)}, bf16[2,8,2,256]{3,1,2,0:T(8,128)(2,1)}, u32[]{:S(2)}) copy-start(bf16[2,8,2,256]{3,1,2,0:T(8,128)(2,1)} %copy-done.58) | copy-start | bytes 49156
  470.4 575.6 %all-gather.31.cloned.1.call-start = ((), (), s32[]{:S(2)}) async-start(), calls=%async_computation.13 | async-start | bytes 1114112 | tf_op jit(solution)/shard_map/all_gather | solution.py:47
  589.4 519.0 %all-gather.37.cloned.1.call-start = ((), (), s32[]{:S(2)}) async-start(), calls=%async_computation.18 | async-start | bytes 3615744 | tf_op jit(solution)/shard_map/all_gather | solution.py:286
  593.4 5.2 copy-start.32
  593.4 5.6 copy-start.61
  598.6 408.2 %copy-start.23 = (bf16[128,2816]{1,0:T(8,128)(2,1)S(1)}, bf16[128,2816]{1,0:T(8,128)(2,1)}, u32[]{:S(2)}) copy-start(bf16[128,2816]{1,0:T(8,128)(2,1)} %get-tuple-element.102) | copy-start | bytes 2162692
  600.4 553.1 %all-gather.35.cloned.1.call-start = ((), (), s32[]{:S(2)}) async-start(), calls=%async_computation.17 | async-start | bytes 3063808 | tf_op jit(solution)/shard_map/all_gather | solution.py:47
  733.9 465.9 %all-gather.29.cloned.1.call-start = ((), (), s32[]{:S(2)}) async-start(), calls=%async_computation.11 | async-start | bytes 3342336 | tf_op jit(solution)/shard_map/all_gather | solution.py:47
  850.5 408.5 %all-gather.33.cloned.1.call-start = ((), (), s32[]{:S(2)}) async-start(), calls=%async_computation.15 | async-start | bytes 6127616 | tf_op jit(solution)/shard_map/all_gather | solution.py:47
  1011.1 37.7 %copy-start.25 = (f32[128,1024]{1,0:T(8,128)S(1)}, f32[128,1024]{1,0:T(8,128)}, u32[]{:S(2)}) copy-start(f32[128,1024]{1,0:T(8,128)} %copy-done.24) | copy-start | bytes 1572868
  1011.1 37.7 %copy-start.36 = (bf16[1,128,1024]{2,1,0:T(8,128)(2,1)S(1)}, bf16[1,128,1024]{2,1,0:T(8,128)(2,1)}, u32[]{:S(2)}) copy-start(bf16[1,128,1024]{2,1,0:T(8,128)(2,1)} %param.33) | copy-start | bytes 786436
  1011.1 37.7 %copy-start.80 = (f32[128]{0:T(128)S(1)}, f32[128]{0:T(128)}, u32[]{:S(2)}) copy-start(f32[128]{0:T(128)} %copy-done.79) | copy-start | bytes 1540
  1258.9 8.1 copy-start.1
  (49 other events, 115.0 us)
Sparse Core Ops, SparseCore 0:
  11.5 72.0 all-gather.16
  101.7 49.5 all-gather.18
  154.8 54.8 all-gather.20
  213.0 89.3 all-gather.22
  305.7 65.8 all-gather.24
  400.5 49.0 all-gather.26
  452.5 136.8 reduce-scatter.6
  592.3 141.4 reduce-scatter.10
  739.5 110.9 reduce-scatter.4
  852.6 154.1 reduce-scatter.8
  1009.0 36.9 all-gather.30
  1049.4 58.9 all-gather.36
  1110.7 42.7 all-gather.34
  1155.6 44.0 all-gather.28
  1201.9 56.9 all-gather.32
